TPU v7x, 32 devices: a whole 2x2x4 slice. The times are simulated.
32 devices in a mesh: gx: 4 (over z), gy: 4 (over y, core), gz: 2 (over x).
Axes of the slice: x: 2, y: 2, z: 4, core: 2. Of those that a mesh axis runs over, the one named last changes fastest.
Arguments:
- offset_vector_field: float32 [3, 64, 64, 256], P(None, 'gx', 'gy', 'gz'), may hold values from -2 to 2
- earlier_creep_deformation: float32 [6, 64, 64, 256], P(None, 'gx', 'gy', 'gz'), may hold values from -0.6 to 0.6
- thermal_state: float32 [64, 64, 256], P('gx', 'gy', 'gz'), may hold values from 1 to 2
- rock_mass_per_volume: float32 [64, 64, 256], P('gx', 'gy', 'gz'), may hold values from 0.5 to 1.5
- rupture_band_indicator: int32 [64, 64, 256], P('gx', 'gy', 'gz'), may hold values 0 or 1
Outputs:
- strain_next: float32 [6, 64, 64, 256], P(None, 'gx', 'gy', 'gz')
- momentum_residual: float32 [3, 64, 64, 256], P(None, 'gx', 'gy', 'gz')
All inputs are finite; a program needn't handle non-finite values. No bound on the sum of `rupture_band_indicator` on one device may be relied on, other than what follows from the above.
Results may differ from a plain program's by a relative error of at most 0.00009.
Values sent between devices are 32-bit elements; how exact they have to be, the bound alone decides.
A program may use at most 64 MiB of HBM per device.

v0:
```python
import jax
import jax.numpy as jnp
from jax import lax
from jax.sharding import PartitionSpec as P


def with_halo(value, sides, width):
    for axis, dim in sides:
        size, length = (lax.axis_size(axis), value.shape[dim])
        up = [(i, (i + 1) % size) for i in range(size - 1)]
        down = [(j, i) for i, j in up]
        last = lax.slice_in_dim(value, length - width, length, axis=dim)
        leading = lax.slice_in_dim(value, 0, width, axis=dim)
        before = lax.ppermute(last, axis, up)
        after = lax.ppermute(leading, axis, down)
        value = jnp.concatenate([before, value, after], axis=dim)
    return value


def carried_in(value, axis, combine, identity):
    size, position = (lax.axis_size(axis), lax.axis_index(axis))
    everything = lax.all_gather(value, axis)
    start = jnp.broadcast_to(jnp.asarray(identity, value.dtype), value.shape)

    def lap(k, before):
        reached = k < position
        new = combine(before, everything[k])
        return jnp.where(reached, new, before)

    return lax.fori_loop(0, size, lap, start)


def face_diff(block, direction):
    if direction == 0:
        return (block[2:, 1:-1, 1:-1] - block[:-2, 1:-1, 1:-1]) * 0.5
    if direction == 1:
        return (block[1:-1, 2:, 1:-1] - block[1:-1, :-2, 1:-1]) * 0.5
    return (block[1:-1, 1:-1, 2:] - block[1:-1, 1:-1, :-2]) * 0.5


def stress_of(elastic):
    trace = elastic[0] + elastic[1] + elastic[2]
    return [
        2.0 * elastic[0] + trace,
        2.0 * elastic[1] + trace,
        2.0 * elastic[2] + trace,
        2.0 * elastic[3],
        2.0 * elastic[4],
        2.0 * elastic[5],
    ]


def evolve_deformation(
    deformation_parts,
    earlier_creep_deformation,
    lithostatic_load,
    thermal_state,
    rupture_band_indicator,
):
    traction_matrix = stress_of(
        [deformation_parts[index] - earlier_creep_deformation[index] for index in range(6)]
    )
    mean_stress = (traction_matrix[0] + traction_matrix[1] + traction_matrix[2]) / 3.0
    deviator = [
        traction_matrix[0] - mean_stress,
        traction_matrix[1] - mean_stress,
        traction_matrix[2] - mean_stress,
        traction_matrix[3],
        traction_matrix[4],
        traction_matrix[5],
    ]
    quadratic_scalar_measure = 0.5 * (
        deviator[0] * deviator[0] + deviator[1] * deviator[1] + deviator[2] * deviator[2]
    )
    quadratic_scalar_measure = (
        quadratic_scalar_measure
        + deviator[3] * deviator[3]
        + deviator[4] * deviator[4]
        + deviator[5] * deviator[5]
    )
    rupture_weakening = 1.0 + 7.0 * rupture_band_indicator.astype(jnp.float32)
    weakening_multiplier = (
        0.5
        * rupture_weakening
        * jnp.exp(-(2.0 + 2.0 * lithostatic_load) / thermal_state)
        * quadratic_scalar_measure
    )
    fresh_deformation = jnp.stack(
        [
            earlier_creep_deformation[index] + weakening_multiplier * deviator[index]
            for index in range(6)
        ]
    )
    stress_next = stress_of(
        [deformation_parts[index] - fresh_deformation[index] for index in range(6)]
    )
    return (fresh_deformation, stress_next)


def shards(
    offset_vector_field,
    earlier_creep_deformation,
    thermal_state,
    rock_mass_per_volume,
    rupture_band_indicator,
):
    padded = with_halo(offset_vector_field, (("gx", 1), ("gy", 2), ("gz", 3)), 1)
    gradient = [
        [face_diff(padded[component], direction) for direction in range(3)]
        for component in range(3)
    ]
    deformation_parts = [
        gradient[0][0],
        gradient[1][1],
        gradient[2][2],
        0.5 * (gradient[0][1] + gradient[1][0]),
        0.5 * (gradient[0][2] + gradient[2][0]),
        0.5 * (gradient[1][2] + gradient[2][1]),
    ]
    depth_cells = rock_mass_per_volume.shape[2]
    layers = lax.axis_size("gz")
    total_depth = depth_cells * layers
    depth_index = lax.axis_index("gz") * depth_cells + jnp.arange(depth_cells, dtype=jnp.int32)
    weight = (
        rock_mass_per_volume
        * (1.0 + 2.0 * depth_index.astype(jnp.float32) / total_depth)
        / total_depth
    )
    row_index = jnp.arange(depth_cells, dtype=jnp.int32)[:, None]
    col_index = jnp.arange(depth_cells, dtype=jnp.int32)[None, :]
    triangle = jnp.where(
        row_index < col_index, 1.0, jnp.where(row_index == col_index, 0.5, 0.0)
    ).astype(jnp.float32)
    local_sum = jnp.dot(
        weight.reshape(-1, depth_cells),
        triangle,
        precision=lax.Precision.HIGHEST,
        preferred_element_type=jnp.float32,
    ).reshape(weight.shape)
    column_total = jnp.sum(weight, axis=2)
    above = carried_in(column_total, "gz", jnp.add, jnp.zeros_like(column_total))
    lithostatic_load = above[:, :, None] + local_sum
    fresh_deformation, traction_matrix = evolve_deformation(
        deformation_parts,
        earlier_creep_deformation,
        lithostatic_load,
        thermal_state,
        rupture_band_indicator,
    )
    strike_set = with_halo(
        jnp.stack([traction_matrix[0], traction_matrix[3], traction_matrix[4]]), (("gx", 1),), 1
    )
    dip_set = with_halo(
        jnp.stack([traction_matrix[3], traction_matrix[1], traction_matrix[5]]), (("gy", 2),), 1
    )
    depth_set = with_halo(
        jnp.stack([traction_matrix[4], traction_matrix[5], traction_matrix[2]]), (("gz", 3),), 1
    )
    along_x = (strike_set[:, 2:] - strike_set[:, :-2]) * 0.5
    along_y = (dip_set[:, :, 2:] - dip_set[:, :, :-2]) * 0.5
    along_z = (depth_set[:, :, :, 2:] - depth_set[:, :, :, :-2]) * 0.5
    zeros = jnp.zeros_like(rock_mass_per_volume)
    momentum = along_x + along_y + along_z - jnp.stack([zeros, zeros, 0.5 * rock_mass_per_volume])
    return (fresh_deformation, momentum)


def solution(mesh):
    return jax.shard_map(
        shards,
        mesh=mesh,
        in_specs=(
            P(None, "gx", "gy", "gz"),
            P(None, "gx", "gy", "gz"),
            P("gx", "gy", "gz"),
            P("gx", "gy", "gz"),
            P("gx", "gy", "gz"),
        ),
        out_specs=(P(None, "gx", "gy", "gz"), P(None, "gx", "gy", "gz")),
        check_vma=False,
    )
```

profile of v0, /device:TPU:14, one launch (start us, length us, event | category | flops | bytes accessed | tf_op | source)
XLA Modules:
  0.0 68.3 jit_solution(17907625204552094776)
XLA Ops:
  0.6 0.8 %fusion.45 = (f32[3,1,16,128]{3,2,1,0:T(8,128)S(1)}, f32[3,1,16,128]{3,2,1,0:T(8,128)S(1)}) fusion(f32[3,16,16,128]{3,2,1,0:T(8,128)} %param.7), kind=kLoop, calls=%fused_computation.121 | loop fusion | bytes 98304 | tf_op jit(solution)/shard_map/slice | solution.py:13
  1.4 3.5 %collective-permute-start = (f32[3,1,16,128]{3,2,1,0:T(8,128)S(1)}, f32[3,1,16,128]{3,2,1,0:T(8,128)S(1)}, u32[]{:S(2)}, u32[]{:S(2)}) collective-permute-start(f32[3,1,16,128]{3,2,1,0:T(8,128)S(1)} %get-tuple-element.136), channel_id=1, source_target_pairs={{0,8},{8,16},{16,24},{1,9},{9,17},{17,25},{2,10},{10,18},{18,26},{... | collective-permute-start | bytes 73736 | tf_op jit(solution)/shard_map/ppermute | solution.py:14
  4.9 2.4 %collective-permute-start.1 = (f32[3,1,16,128]{3,2,1,0:T(8,128)S(1)}, f32[3,1,16,128]{3,2,1,0:T(8,128)S(1)}, u32[]{:S(2)}, u32[]{:S(2)}) collective-permute-start(f32[3,1,16,128]{3,2,1,0:T(8,128)S(1)} %get-tuple-element.135), channel_id=1, source_target_pairs={{8,0},{16,8},{24,16},{9,1},{17,9},{25,17},{10,2},{18,10},{26,18},{... | collective-permute-start | bytes 73736 | tf_op jit(solution)/shard_map/ppermute | solution.py:15
  7.3 0.0 collective-permute-done
  7.3 1.0 %constant_dynamic-update-slice_fusion.1 = f32[3,18,16,128]{3,2,1,0:T(8,128)S(1)} fusion(f32[3,18,16,128]{3,2,1,0:T(8,128)S(1)} %constant_dynamic-update-slice_fusion.2, f32[3,16,16,128]{3,2,1,0:T(8,128)} %param.7), kind=kLoop, calls=%fused_computation.111 | loop fusion | bytes 786432
  8.3 2.3 %collective-permute-done.1 = f32[3,1,16,128]{3,2,1,0:T(8,128)S(1)} collective-permute-done((f32[3,1,16,128]{3,2,1,0:T(8,128)S(1)}, f32[3,1,16,128]{3,2,1,0:T(8,128)S(1)}, u32[]{:S(2)}, u32[]{:S(2)}) %collective-permute-start.1) | collective-permute-done | bytes 24608 | tf_op jit(solution)/shard_map/ppermute | solution.py:15
  10.6 1.9 %collective-permute-start.2 = (f32[3,18,1,128]{3,2,1,0:T(1,128)S(1)}, f32[3,18,1,128]{3,2,1,0:T(1,128)S(1)}, u32[]{:S(2)}, u32[]{:S(2)}) collective-permute-start(f32[3,18,1,128]{3,2,1,0:T(1,128)S(1)} %get-tuple-element.127), channel_id=1, source_target_pairs={{0,2},{2,4},{4,6},{1,3},{3,5},{5,7},{8,10},{10,12},{12,14},{9,11},... | collective-permute-start | bytes 82952 | tf_op jit(solution)/shard_map/ppermute | solution.py:14
  12.6 3.6 %collective-permute-start.3 = (f32[3,18,1,128]{3,2,1,0:T(1,128)S(1)}, f32[3,18,1,128]{3,2,1,0:T(1,128)S(1)}, u32[]{:S(2)}, u32[]{:S(2)}) collective-permute-start(f32[3,18,1,128]{3,2,1,0:T(1,128)S(1)} %get-tuple-element.128), channel_id=1, source_target_pairs={{2,0},{4,2},{6,4},{3,1},{5,3},{7,5},{10,8},{12,10},{14,12},{11,9},... | collective-permute-start | bytes 82952 | tf_op jit(solution)/shard_map/ppermute | solution.py:15
  16.2 1.0 %multiply_bitcast_fusion = (f32[1,16,16,128]{3,2,1,0:T(8,128)S(1)}, f32[16,16]{1,0:T(8,128)S(1)}) fusion(f32[16,16,128]{2,1,0:T(8,128)} %param.10, f32[128]{0:T(128)S(1)} %multiply_add_fusion.3), kind=kLoop, calls=%fused_computation.79 | loop fusion | flops 130816 | bytes 263680 | tf_op jit(solution)/shard_map/stack | solution.py:163
  17.3 4.4 %all-gather = f32[32,16]{1,0:T(8,128)S(1)} all-gather(f32[16,16]{1,0:T(8,128)S(1)} %get-tuple-element.138), channel_id=2, replica_groups=mesh['gx'=4,'gy'=4,'gz'=2] {'gz'}, dimensions={0}, use_global_device_ids=true | all-gather | bytes 3072 | tf_op jit(solution)/shard_map/all_gather | solution.py:22
  21.6 0.0 collective-permute-done.2
  21.6 0.0 collective-permute-done.3
  21.6 0.1 pad_maximum_fusion.1
  21.7 0.2 fusion.42
  22.0 0.4 copy.8
  22.4 2.4 %collective-permute-start.5 = (f32[3,18,18,1]{2,3,1,0:T(1,128)S(1)}, f32[3,18,18,1]{2,3,1,0:T(1,128)S(1)}, u32[]{:S(2)}, u32[]{:S(2)}) collective-permute-start(f32[3,18,18,1]{2,3,1,0:T(1,128)S(1)} %copy.8), channel_id=1, source_target_pairs={{1,0},{3,2},{5,4},{7,6},{9,8},{11,10},{13,12},{15,14},{17,16},{19,... | collective-permute-start | bytes 11672 | tf_op jit(solution)/shard_map/ppermute | solution.py:15
  24.8 0.4 copy.7
  25.3 1.3 %collective-permute-start.4 = (f32[3,18,18,1]{2,3,1,0:T(1,128)S(1)}, f32[3,18,18,1]{2,3,1,0:T(1,128)S(1)}, u32[]{:S(2)}, u32[]{:S(2)}) collective-permute-start(f32[3,18,18,1]{2,3,1,0:T(1,128)S(1)} %copy.7), channel_id=1, source_target_pairs={{0,1},{2,3},{4,5},{6,7},{8,9},{10,11},{12,13},{14,15},{16,17},{18,... | collective-permute-start | bytes 11672 | tf_op jit(solution)/shard_map/ppermute | solution.py:14
  26.5 0.1 while.14
  26.6 0.0 collective-permute-done.5
  26.6 0.4 copy.10
  27.1 3.9 %collective-permute-done.4 = f32[3,18,18,1]{2,3,1,0:T(1,128)S(1)} collective-permute-done((f32[3,18,18,1]{2,3,1,0:T(1,128)S(1)}, f32[3,18,18,1]{2,3,1,0:T(1,128)S(1)}, u32[]{:S(2)}, u32[]{:S(2)}) %collective-permute-start.4) | collective-permute-done | bytes 3920 | tf_op jit(solution)/shard_map/ppermute | solution.py:14
  31.0 0.4 copy.9
  31.4 0.8 %pad_maximum_fusion = f32[3,18,18,130]{3,2,1,0:T(8,128)S(1)} fusion(f32[3,18,18,1]{3,2,1,0:T(8,128)S(1)} %copy.10, f32[3,18,1,128]{3,2,1,0:T(1,128)S(1)} %collective-permute-done.3, f32[3,18,16,128]{3,2,1,0:T(8,128)S(1)} %constant_dynamic-update-slice_fusion, f32[3,18,1,128]{3,2,1,0:T(1,128)S(1)} %collective-permute-done.2, f32[3,18,18,1]{3,2,1,0:T(8,128)S(1)} %copy.9), kind=kLoop, calls=%fused_computation.1 | loop fusion | flops 505440 | bytes 1010880 | tf_op jit(solution)/shard_map/concatenate | solution.py:16
  32.3 0.0 copy-start
  32.3 0.1 slice_bitcast_fusion.2
  32.4 1.0 %copy-done = f32[6,16,16,128]{3,2,1,0:T(8,128)S(1)} copy-done((f32[6,16,16,128]{3,2,1,0:T(8,128)S(1)}, f32[6,16,16,128]{3,2,1,0:T(8,128)}, u32[]{:S(2)}) %copy-start) | copy-done | bytes 786456
  33.4 0.5 multiply_add_fusion.2
  33.9 0.0 copy-start.1
  33.9 0.0 copy-start.3
  33.9 0.0 copy-start.4
  33.9 0.2 multiply_add_fusion.1
  34.1 0.7 %copy-done.1 = f32[16,16,128]{2,1,0:T(8,128)S(1)} copy-done((f32[16,16,128]{2,1,0:T(8,128)S(1)}, f32[16,16,128]{2,1,0:T(8,128)}, u32[]{:S(2)}) %copy-start.1) | copy-done | bytes 131096
  34.8 0.1 copy-done.3
  34.9 0.1 copy-done.4
  34.9 0.4 fusion.6
  35.3 0.2 add_bitcast_fusion.2
  35.5 2.4 %collective-permute-start.6 = (f32[3,1,16,128]{3,2,1,0:T(8,128)S(1)}, f32[3,1,16,128]{3,2,1,0:T(8,128)S(1)}, u32[]{:S(2)}, u32[]{:S(2)}) collective-permute-start(f32[3,1,16,128]{3,2,1,0:T(8,128)S(1)} %get-tuple-element.129), channel_id=1, source_target_pairs={{8,0},{16,8},{24,16},{9,1},{17,9},{25,17},{10,2},{18,10},{26,18},{... | collective-permute-start | bytes 73736 | tf_op jit(solution)/shard_map/ppermute | solution.py:15
  37.9 3.5 %collective-permute-start.7 = (f32[3,1,16,128]{3,2,1,0:T(8,128)S(1)}, f32[3,1,16,128]{3,2,1,0:T(8,128)S(1)}, u32[]{:S(2)}, u32[]{:S(2)}) collective-permute-start(f32[3,1,16,128]{3,2,1,0:T(8,128)S(1)} %get-tuple-element.130), channel_id=1, source_target_pairs={{0,8},{8,16},{16,24},{1,9},{9,17},{17,25},{2,10},{10,18},{18,26},{... | collective-permute-start | bytes 73736 | tf_op jit(solution)/shard_map/ppermute | solution.py:14
  41.5 1.9 %collective-permute-start.8 = (f32[3,16,1,128]{3,2,1,0:T(1,128)S(1)}, f32[3,16,1,128]{3,2,1,0:T(1,128)S(1)}, u32[]{:S(2)}, u32[]{:S(2)}) collective-permute-start(f32[3,16,1,128]{3,2,1,0:T(1,128)S(1)} %get-tuple-element.131), channel_id=1, source_target_pairs={{2,0},{4,2},{6,4},{3,1},{5,3},{7,5},{10,8},{12,10},{14,12},{11,9},... | collective-permute-start | bytes 73736 | tf_op jit(solution)/shard_map/ppermute | solution.py:15
  43.4 2.4 %collective-permute-start.9 = (f32[3,16,1,128]{3,2,1,0:T(1,128)S(1)}, f32[3,16,1,128]{3,2,1,0:T(1,128)S(1)}, u32[]{:S(2)}, u32[]{:S(2)}) collective-permute-start(f32[3,16,1,128]{3,2,1,0:T(1,128)S(1)} %get-tuple-element.132), channel_id=1, source_target_pairs={{0,2},{2,4},{4,6},{1,3},{3,5},{5,7},{8,10},{10,12},{12,14},{9,11},... | collective-permute-start | bytes 73736 | tf_op jit(solution)/shard_map/ppermute | solution.py:14
  45.8 0.2 fusion.44
  46.0 1.6 %collective-permute-start.10 = (f32[3,16,16,1]{3,2,1,0:T(8,128)S(1)}, f32[3,16,16,1]{3,2,1,0:T(8,128)S(1)}, u32[]{:S(2)}, u32[]{:S(2)}) collective-permute-start(f32[3,16,16,1]{3,2,1,0:T(8,128)S(1)} %get-tuple-element.133), channel_id=1, source_target_pairs={{1,0},{3,2},{5,4},{7,6},{9,8},{11,10},{13,12},{15,14},{17,16},{19,... | collective-permute-start | bytes 9224 | tf_op jit(solution)/shard_map/ppermute | solution.py:15
  47.8 7.7 %collective-permute-done.10 = f32[3,16,16,1]{3,2,1,0:T(8,128)S(1)} collective-permute-done((f32[3,16,16,1]{3,2,1,0:T(8,128)S(1)}, f32[3,16,16,1]{3,2,1,0:T(8,128)S(1)}, u32[]{:S(2)}, u32[]{:S(2)}) %collective-permute-start.10) | collective-permute-done | bytes 3104 | tf_op jit(solution)/shard_map/ppermute | solution.py:15
  55.6 1.3 %collective-permute-start.11 = (f32[3,16,16,1]{3,2,1,0:T(8,128)S(1)}, f32[3,16,16,1]{3,2,1,0:T(8,128)S(1)}, u32[]{:S(2)}, u32[]{:S(2)}) collective-permute-start(f32[3,16,16,1]{3,2,1,0:T(8,128)S(1)} %get-tuple-element.134), channel_id=1, source_target_pairs={{0,1},{2,3},{4,5},{6,7},{8,9},{10,11},{12,13},{14,15},{16,17},{18,... | collective-permute-start | bytes 9224 | tf_op jit(solution)/shard_map/ppermute | solution.py:14
  56.9 0.0 copy-start.2
  56.9 10.2 %collective-permute-done.11 = f32[3,16,16,1]{3,2,1,0:T(8,128)S(1)} collective-permute-done((f32[3,16,16,1]{3,2,1,0:T(8,128)S(1)}, f32[3,16,16,1]{3,2,1,0:T(8,128)S(1)}, u32[]{:S(2)}, u32[]{:S(2)}) %collective-permute-start.11) | collective-permute-done | bytes 3104 | tf_op jit(solution)/shard_map/ppermute | solution.py:14
  67.1 0.0 collective-permute-done.6
  67.1 0.0 collective-permute-done.7
  67.1 0.0 collective-permute-done.8
  67.1 0.0 collective-permute-done.9
  67.1 1.1 %fusion.10 = f32[3,16,16,128]{3,2,1,0:T(8,128)} fusion(f32[3,16,16,1]{3,2,1,0:T(8,128)S(1)} %collective-permute-done.11, f32[1,16,16,128]{3,2,1,0:T(8,128)S(1)} %get-tuple-element.140, f32[1,16,16,128]{3,2,1,0:T(8,128)S(1)} %get-tuple-element.120, f32[1,16,16,128]{3,2,1,0:T(8,128)S(1)} %get-tuple-element.119, ...), kind=kLoop, calls=%fused_computation.18 | loop fusion | flops 2457600 | bytes 1415168 | tf_op jit(solution)/shard_map/sub | solution.py:163
  68.3 0.0 copy-done.2
  (17 shorter events, 0.3 us)
Async XLA Ops:
  1.4 5.9 %collective-permute-start = (f32[3,1,16,128]{3,2,1,0:T(8,128)S(1)}, f32[3,1,16,128]{3,2,1,0:T(8,128)S(1)}, u32[]{:S(2)}, u32[]{:S(2)}) collective-permute-start(f32[3,1,16,128]{3,2,1,0:T(8,128)S(1)} %get-tuple-element.136), channel_id=1, source_target_pairs={{0,8},{8,16},{16,24},{1,9},{9,17},{17,25},{2,10},{10,18},{18,26},{... | collective-permute-start | bytes 73736 | tf_op jit(solution)/shard_map/ppermute | solution.py:14
  4.9 5.7 %collective-permute-start.1 = (f32[3,1,16,128]{3,2,1,0:T(8,128)S(1)}, f32[3,1,16,128]{3,2,1,0:T(8,128)S(1)}, u32[]{:S(2)}, u32[]{:S(2)}) collective-permute-start(f32[3,1,16,128]{3,2,1,0:T(8,128)S(1)} %get-tuple-element.135), channel_id=1, source_target_pairs={{8,0},{16,8},{24,16},{9,1},{17,9},{25,17},{10,2},{18,10},{26,18},{... | collective-permute-start | bytes 73736 | tf_op jit(solution)/shard_map/ppermute | solution.py:15
  10.6 11.0 %collective-permute-start.2 = (f32[3,18,1,128]{3,2,1,0:T(1,128)S(1)}, f32[3,18,1,128]{3,2,1,0:T(1,128)S(1)}, u32[]{:S(2)}, u32[]{:S(2)}) collective-permute-start(f32[3,18,1,128]{3,2,1,0:T(1,128)S(1)} %get-tuple-element.127), channel_id=1, source_target_pairs={{0,2},{2,4},{4,6},{1,3},{3,5},{5,7},{8,10},{10,12},{12,14},{9,11},... | collective-permute-start | bytes 82952 | tf_op jit(solution)/shard_map/ppermute | solution.py:14
  12.6 9.0 %collective-permute-start.3 = (f32[3,18,1,128]{3,2,1,0:T(1,128)S(1)}, f32[3,18,1,128]{3,2,1,0:T(1,128)S(1)}, u32[]{:S(2)}, u32[]{:S(2)}) collective-permute-start(f32[3,18,1,128]{3,2,1,0:T(1,128)S(1)} %get-tuple-element.128), channel_id=1, source_target_pairs={{2,0},{4,2},{6,4},{3,1},{5,3},{7,5},{10,8},{12,10},{14,12},{11,9},... | collective-permute-start | bytes 82952 | tf_op jit(solution)/shard_map/ppermute | solution.py:15
  22.4 4.2 %collective-permute-start.5 = (f32[3,18,18,1]{2,3,1,0:T(1,128)S(1)}, f32[3,18,18,1]{2,3,1,0:T(1,128)S(1)}, u32[]{:S(2)}, u32[]{:S(2)}) collective-permute-start(f32[3,18,18,1]{2,3,1,0:T(1,128)S(1)} %copy.8), channel_id=1, source_target_pairs={{1,0},{3,2},{5,4},{7,6},{9,8},{11,10},{13,12},{15,14},{17,16},{19,... | collective-permute-start | bytes 11672 | tf_op jit(solution)/shard_map/ppermute | solution.py:15
  25.3 5.7 %collective-permute-start.4 = (f32[3,18,18,1]{2,3,1,0:T(1,128)S(1)}, f32[3,18,18,1]{2,3,1,0:T(1,128)S(1)}, u32[]{:S(2)}, u32[]{:S(2)}) collective-permute-start(f32[3,18,18,1]{2,3,1,0:T(1,128)S(1)} %copy.7), channel_id=1, source_target_pairs={{0,1},{2,3},{4,5},{6,7},{8,9},{10,11},{12,13},{14,15},{16,17},{18,... | collective-permute-start | bytes 11672 | tf_op jit(solution)/shard_map/ppermute | solution.py:14
  32.3 1.1 %copy-start = (f32[6,16,16,128]{3,2,1,0:T(8,128)S(1)}, f32[6,16,16,128]{3,2,1,0:T(8,128)}, u32[]{:S(2)}) copy-start(f32[6,16,16,128]{3,2,1,0:T(8,128)} %param.8) | copy-start | bytes 2359300
  33.9 0.9 %copy-start.1 = (f32[16,16,128]{2,1,0:T(8,128)S(1)}, f32[16,16,128]{2,1,0:T(8,128)}, u32[]{:S(2)}) copy-start(f32[16,16,128]{2,1,0:T(8,128)} %param.10) | copy-start | bytes 393220
  33.9 1.0 %copy-start.3 = (f32[16,16,128]{2,1,0:T(8,128)S(1)}, f32[16,16,128]{2,1,0:T(8,128)}, u32[]{:S(2)}) copy-start(f32[16,16,128]{2,1,0:T(8,128)} %param.9) | copy-start | bytes 393220
  33.9 1.0 %copy-start.4 = (s32[16,16,128]{2,1,0:T(8,128)S(1)}, s32[16,16,128]{2,1,0:T(8,128)}, u32[]{:S(2)}) copy-start(s32[16,16,128]{2,1,0:T(8,128)} %param.11) | copy-start | bytes 393220
  35.5 31.6 %collective-permute-start.6 = (f32[3,1,16,128]{3,2,1,0:T(8,128)S(1)}, f32[3,1,16,128]{3,2,1,0:T(8,128)S(1)}, u32[]{:S(2)}, u32[]{:S(2)}) collective-permute-start(f32[3,1,16,128]{3,2,1,0:T(8,128)S(1)} %get-tuple-element.129), channel_id=1, source_target_pairs={{8,0},{16,8},{24,16},{9,1},{17,9},{25,17},{10,2},{18,10},{26,18},{... | collective-permute-start | bytes 73736 | tf_op jit(solution)/shard_map/ppermute | solution.py:15
  37.9 29.2 %collective-permute-start.7 = (f32[3,1,16,128]{3,2,1,0:T(8,128)S(1)}, f32[3,1,16,128]{3,2,1,0:T(8,128)S(1)}, u32[]{:S(2)}, u32[]{:S(2)}) collective-permute-start(f32[3,1,16,128]{3,2,1,0:T(8,128)S(1)} %get-tuple-element.130), channel_id=1, source_target_pairs={{0,8},{8,16},{16,24},{1,9},{9,17},{17,25},{2,10},{10,18},{18,26},{... | collective-permute-start | bytes 73736 | tf_op jit(solution)/shard_map/ppermute | solution.py:14
  41.5 25.6 %collective-permute-start.8 = (f32[3,16,1,128]{3,2,1,0:T(1,128)S(1)}, f32[3,16,1,128]{3,2,1,0:T(1,128)S(1)}, u32[]{:S(2)}, u32[]{:S(2)}) collective-permute-start(f32[3,16,1,128]{3,2,1,0:T(1,128)S(1)} %get-tuple-element.131), channel_id=1, source_target_pairs={{2,0},{4,2},{6,4},{3,1},{5,3},{7,5},{10,8},{12,10},{14,12},{11,9},... | collective-permute-start | bytes 73736 | tf_op jit(solution)/shard_map/ppermute | solution.py:15
  43.4 23.7 %collective-permute-start.9 = (f32[3,16,1,128]{3,2,1,0:T(1,128)S(1)}, f32[3,16,1,128]{3,2,1,0:T(1,128)S(1)}, u32[]{:S(2)}, u32[]{:S(2)}) collective-permute-start(f32[3,16,1,128]{3,2,1,0:T(1,128)S(1)} %get-tuple-element.132), channel_id=1, source_target_pairs={{0,2},{2,4},{4,6},{1,3},{3,5},{5,7},{8,10},{10,12},{12,14},{9,11},... | collective-permute-start | bytes 73736 | tf_op jit(solution)/shard_map/ppermute | solution.py:14
  46.0 9.5 %collective-permute-start.10 = (f32[3,16,16,1]{3,2,1,0:T(8,128)S(1)}, f32[3,16,16,1]{3,2,1,0:T(8,128)S(1)}, u32[]{:S(2)}, u32[]{:S(2)}) collective-permute-start(f32[3,16,16,1]{3,2,1,0:T(8,128)S(1)} %get-tuple-element.133), channel_id=1, source_target_pairs={{1,0},{3,2},{5,4},{7,6},{9,8},{11,10},{13,12},{15,14},{17,16},{19,... | collective-permute-start | bytes 9224 | tf_op jit(solution)/shard_map/ppermute | solution.py:15
  55.6 11.5 %collective-permute-start.11 = (f32[3,16,16,1]{3,2,1,0:T(8,128)S(1)}, f32[3,16,16,1]{3,2,1,0:T(8,128)S(1)}, u32[]{:S(2)}, u32[]{:S(2)}) collective-permute-start(f32[3,16,16,1]{3,2,1,0:T(8,128)S(1)} %get-tuple-element.134), channel_id=1, source_target_pairs={{0,1},{2,3},{4,5},{6,7},{8,9},{10,11},{12,13},{14,15},{16,17},{18,... | collective-permute-start | bytes 9224 | tf_op jit(solution)/shard_map/ppermute | solution.py:14
  56.9 11.4 %copy-start.2 = (f32[6,16,16,128]{3,2,1,0:T(8,128)}, f32[6,16,16,128]{3,2,1,0:T(8,128)S(1)}, u32[]{:S(2)}) copy-start(f32[6,16,16,128]{3,2,1,0:T(8,128)S(1)} %bitcast_dynamic-update-slice_fusion) | copy-start | bytes 2359300
where the time goes:
time: 68.8 us; the launch traced here: 68.3 us
  starting transfers between devices  28.2 us (41%)
  waiting for transfers between devices  24.2 us (35%)
  local copies, waits for them, and re-layouts  5.99 us (9%)
  blocking collectives  4.36 us (6%)
  other arithmetic  4.18 us (6%)
  between operations  0.97 us (1%)
    ppermute x6, starting transfers between devices, with_halo(): after = lax.ppermute(leading, axis, down)  14.3 us
    ppermute x6, waiting for transfers between devices, with_halo(): before = lax.ppermute(last, axis, up)  14.1 us
    ppermute x6, starting transfers between devices, with_halo(): before = lax.ppermute(last, axis, up)  13.8 us
    ppermute x6, waiting for transfers between devices, with_halo(): after = lax.ppermute(leading, axis, down)  10 us
    all_gather x1, blocking collectives, carried_in(): everything = lax.all_gather(value, axis)  4.36 us
    unnamed x15, local copies, waits for them, and re-layouts  2.93 us
  transfers between devices with their start and end apart: 12, of which 4 were waited for; matrix products, arithmetic and copies ran while one was open for 5% of the time, Pallas kernels for 0%

commit v1 on v0

v1 whole, which is shorter than its diff:
```python
import functools

import jax
import jax.numpy as jnp
from jax import lax
from jax.experimental import pallas as pl
from jax.experimental.pallas import tpu as pltpu
from jax.sharding import PartitionSpec as P

MESH = pl.DeviceIdType.MESH
AXES = ("gx", "gy", "gz")
X_SET = (0, 2, 1)
Y_SET = (2, 3, 4)
Z_SET = (1, 4, 5)


def kernel(
    dims, sizes,
    u_hbm, e_hbm, t_hbm, r_hbm, b_hbm,
    f_hbm, m_hbm,
    uv, ev, tv, rv, bv, pv, el, nt, fv, mv, sp,
    yus, yur, zus, zur, zuh, xur, yss, ysr, zss, zsr, xsr,
    in_sem, out_sem, x_send, x_recv, y_send, y_recv, z_send, z_recv,
    x2_send, x2_recv, y2_send, y2_recv, z2_send, z2_recv,
):
    X, Y, Z = dims
    N = X * Y
    layers = sizes[2]
    me = [lax.axis_index(a) for a in AXES]
    has = [(me[a] > 0, me[a] < sizes[a] - 1) for a in range(3)]

    def to(axis, step):
        return {AXES[axis]: me[axis] + step}

    loads = [
        pltpu.make_async_copy(src, dst, in_sem.at[i])
        for i, (src, dst) in enumerate(
            (
                (r_hbm, rv),
                (u_hbm, uv.at[:, pl.ds(Y, N), :]),
                (e_hbm, ev),
                (t_hbm, tv),
                (b_hbm, bv),
            )
        )
    ]
    for copy in loads:
        copy.start()

    barrier = pltpu.get_barrier_semaphore()
    expected = jnp.int32(0)
    for axis in range(3):
        for side, step in enumerate((-1, 1)):
            expected = expected + has[axis][side].astype(jnp.int32)

            @pl.when(has[axis][side])
            def _(axis=axis, step=step):
                pl.semaphore_signal(barrier, inc=1, device_id=to(axis, step), device_id_type=MESH)

    for d in range(2, layers):
        expected = expected + (me[2] + d < layers).astype(jnp.int32)

        @pl.when(me[2] >= d)
        def _(d=d):
            pl.semaphore_signal(barrier, inc=1, device_id=to(2, -d), device_id_type=MESH)

    plane = jnp.zeros((Y, Z), jnp.float32)
    for c in range(3):
        uv[c, pl.ds(0, Y), :] = plane
        uv[c, pl.ds(Y + N, Y), :] = plane
    for c in range(6):
        sp[c, pl.ds(0, Y), :] = plane
        sp[c, pl.ds(Y + N, Y), :] = plane
    for d in range(1, layers):
        @pl.when(me[2] < d)
        def _(d=d):
            zur[d - 1] = plane

    @pl.when(jnp.logical_not(has[2][0]))
    def _():
        zsr[0] = plane

    @pl.when(jnp.logical_not(has[2][1]))
    def _():
        zuh[...] = plane
        zsr[1] = plane

    lane = lax.broadcasted_iota(jnp.int32, (Y, Z), 1)
    row = lax.broadcasted_iota(jnp.int32, (Y, Z), 0)
    pair = lane >> 1
    even = (lane & 1) == 0
    not_last = jnp.where(row < Y - 1, 0.5, 0.0).astype(jnp.float32)
    not_first = jnp.where(row > 0, 0.5, 0.0).astype(jnp.float32)
    z_first = jnp.where(lane > 0, 0.5, 0.0).astype(jnp.float32)
    z_last = jnp.where(lane < Z - 1, 0.5, 0.0).astype(jnp.float32)
    z_edge = jnp.where(lane == 0, -0.5, jnp.where(lane == Z - 1, 0.5, 0.0)).astype(jnp.float32)

    loads[0].wait()
    total_depth = Z * layers
    depth = (me[2] * Z + lax.broadcasted_iota(jnp.int32, (N, Z), 1)).astype(jnp.float32)
    weight = rv[...] * (1.0 + 2.0 * depth / total_depth) / total_depth
    above_row = lax.broadcasted_iota(jnp.int32, (Z, 2 * Z), 0)
    column = lax.broadcasted_iota(jnp.int32, (Z, 2 * Z), 1)
    triangle = jnp.where(
        (above_row < column) | (column >= Z),
        1.0,
        jnp.where(above_row == column, 0.5, 0.0),
    ).astype(jnp.float32)
    sums = jnp.dot(
        weight, triangle, precision=lax.Precision.HIGHEST, preferred_element_type=jnp.float32
    )
    pv[...] = sums[:, :Z] + 1.0
    totals = sums[:, Z:]

    loads[1].wait()
    for side, y in enumerate((0, Y - 1)):
        for c in range(3):
            yus[side, c] = uv[c, pl.ds(Y + y, X, stride=Y), :]
    message = plane
    for x in range(X):
        for c in range(3):
            q = c * X + x
            tile = pltpu.roll(uv[c, pl.ds(Y + x * Y, Y), :], (2 * q + 1) % Z, 1)
            message = jnp.where(pair == q, tile, message)
        message = jnp.where(pair == 3 * X + x, totals[x * Y:(x + 1) * Y], message)
    zus[...] = message

    pl.semaphore_wait(barrier, expected)

    def remote(src, dst, send, recv, axis, step):
        return pltpu.make_async_remote_copy(
            src_ref=src, dst_ref=dst, send_sem=send, recv_sem=recv,
            device_id=to(axis, step), device_id_type=MESH,
        )

    first = []
    for side, step in enumerate((-1, 1)):
        other = 1 - side
        edge = Y if side == 0 else Y * X
        first.append((has[0][side], has[0][other], remote(
            uv.at[:, pl.ds(edge, Y), :], xur.at[other], x_send.at[side], x_recv.at[other], 0, step)))
        first.append((has[1][side], has[1][other], remote(
            yus.at[side], yur.at[other], y_send.at[side], y_recv.at[other], 1, step)))
    first.append((has[2][0], has[2][1], remote(zus, zuh, z_send.at[0], z_recv.at[0], 2, -1)))
    for d in range(1, layers):
        first.append((me[2] + d < layers, me[2] >= d, remote(
            zus, zur.at[d - 1], z_send.at[d], z_recv.at[d], 2, d)))
    for sends, _, copy in first:
        @pl.when(sends)
        def _(copy=copy):
            copy.start()

    for copy in loads[2:]:
        copy.wait()
    for x in range(X):
        base = Y + x * Y
        own = pl.ds(x * Y, Y)
        grad = []
        for c in range(3):
            here = uv[c, pl.ds(base, Y), :]
            grad.append((
                (uv[c, pl.ds(base + Y, Y), :] - uv[c, pl.ds(base - Y, Y), :]) * 0.5,
                uv[c, pl.ds(base + 1, Y), :] * not_last - uv[c, pl.ds(base - 1, Y), :] * not_first,
                pltpu.roll(here, Z - 1, 1) * z_last - pltpu.roll(here, 1, 1) * z_first,
            ))
        el[0, own, :] = grad[0][0] - ev[0, own, :]
        el[1, own, :] = grad[1][1] - ev[1, own, :]
        el[2, own, :] = grad[2][2] - ev[2, own, :]
        el[3, own, :] = 0.5 * (grad[0][1] + grad[1][0]) - ev[3, own, :]
        el[4, own, :] = 0.5 * (grad[0][2] + grad[2][0]) - ev[4, own, :]
        el[5, own, :] = 0.5 * (grad[1][2] + grad[2][1]) - ev[5, own, :]
        nt[own, :] = -2.0 / tv[own, :]

    for (_, receives, copy) in first:
        @pl.when(receives)
        def _(copy=copy):
            copy.wait_recv()

    for side in range(2):
        sign = -1.0 if side == 0 else 1.0
        at = 0 if side == 0 else X - 1
        line = 0 if side == 0 else Y - 1

        @pl.when(has[0][side])
        def _(side=side, sign=sign, at=at):
            own = pl.ds(at * Y, Y)
            for c, (part, factor) in enumerate(((0, 0.5), (3, 0.25), (4, 0.25))):
                el[part, own, :] = el[part, own, :] + (sign * factor) * xur[side, c]

        @pl.when(has[1][side])
        def _(side=side, sign=sign, line=line):
            own = pl.ds(line, X, stride=Y)
            for c, (part, factor) in enumerate(((3, 0.25), (1, 0.5), (5, 0.25))):
                el[part, own, :] = el[part, own, :] + (sign * factor) * yur[side, c]

    low = zur[0] if layers > 1 else plane
    carried = low
    for d in range(2, layers):
        carried = carried + zur[d - 1]
    merged = jnp.where(even, low, pltpu.roll(zuh[...], Z - 2, 1))

    def edge_term(tile, q):
        return (pltpu.roll(tile, (Z - 2 * q) % Z, 1) if q else tile) * z_edge

    message = plane
    for x in [0, X - 1] + list(range(1, X - 1)):
        own = pl.ds(x * Y, Y)
        e = [el[c, own, :] for c in range(6)]
        e[4] = e[4] + 0.5 * edge_term(merged, x)
        e[5] = e[5] + 0.5 * edge_term(merged, X + x)
        e[2] = e[2] + edge_term(merged, 2 * X + x)
        at = 2 * (3 * X + x)
        load = pv[own, :] + jnp.broadcast_to(carried[:, at:at + 1], (Y, Z))
        trace = e[0] + e[1] + e[2]
        third = trace * (1.0 / 3.0)
        dev = [2.0 * (e[c] - third) for c in range(3)] + [2.0 * e[c] for c in range(3, 6)]
        second = 0.5 * (dev[0] * dev[0] + dev[1] * dev[1] + dev[2] * dev[2])
        second = second + dev[3] * dev[3] + dev[4] * dev[4] + dev[5] * dev[5]
        weak = 0.5 + 3.5 * bv[own, :].astype(jnp.float32)
        rate = weak * jnp.exp(load * nt[own, :]) * second
        for c in range(6):
            step = rate * dev[c]
            fv[c, own, :] = ev[c, own, :] + step
            e[c] = e[c] - step
        trace = e[0] + e[1] + e[2]
        stress = [
            2.0 * e[0] + trace, 2.0 * e[4], 2.0 * e[3],
            2.0 * e[1] + trace, 2.0 * e[5], 2.0 * e[2] + trace,
        ]
        for c in range(6):
            sp[c, pl.ds(Y + x * Y, Y), :] = stress[c]
        for c in range(3):
            q = c * X + x
            message = jnp.where(pair == q, pltpu.roll(stress[Z_SET[c]], (2 * q + 1) % Z, 1), message)
    zss[...] = message
    for side, y in enumerate((0, Y - 1)):
        for c in range(3):
            yss[side, c] = sp[2 + c, pl.ds(Y + y, X, stride=Y), :]

    second_set = []
    for side, step in enumerate((-1, 1)):
        other = 1 - side
        edge = Y if side == 0 else Y * X
        second_set.append((has[0][side], has[0][other], remote(
            sp.at[pl.ds(0, 3), pl.ds(edge, Y), :], xsr.at[other], x2_send.at[side], x2_recv.at[other], 0, step)))
        second_set.append((has[1][side], has[1][other], remote(
            yss.at[side], ysr.at[other], y2_send.at[side], y2_recv.at[other], 1, step)))
        second_set.append((has[2][side], has[2][other], remote(
            zss, zsr.at[other], z2_send.at[side], z2_recv.at[other], 2, step)))
    for sends, _, copy in second_set:
        @pl.when(sends)
        def _(copy=copy):
            copy.start()
    strain_out = pltpu.make_async_copy(fv, f_hbm, out_sem.at[0])
    strain_out.start()

    for x in range(X):
        base = Y + x * Y
        own = pl.ds(x * Y, Y)
        for c in range(3):
            cx, cy, cz = X_SET[c], Y_SET[c], Z_SET[c]
            here = sp[cz, pl.ds(base, Y), :]
            total = (sp[cx, pl.ds(base + Y, Y), :] - sp[cx, pl.ds(base - Y, Y), :]) * 0.5
            total = total + (
                sp[cy, pl.ds(base + 1, Y), :] * not_last - sp[cy, pl.ds(base - 1, Y), :] * not_first
            )
            total = total + (pltpu.roll(here, Z - 1, 1) * z_last - pltpu.roll(here, 1, 1) * z_first)
            if c == 2:
                total = total - 0.5 * rv[own, :]
            mv[c, own, :] = total

    for (_, receives, copy) in second_set:
        @pl.when(receives)
        def _(copy=copy):
            copy.wait_recv()

    for side in range(2):
        factor = -0.5 if side == 0 else 0.5
        at = 0 if side == 0 else X - 1
        line = 0 if side == 0 else Y - 1

        @pl.when(has[0][side])
        def _(side=side, factor=factor, at=at):
            own = pl.ds(at * Y, Y)
            for c in range(3):
                mv[c, own, :] = mv[c, own, :] + factor * xsr[side, X_SET[c]]

        @pl.when(has[1][side])
        def _(side=side, factor=factor, line=line):
            own = pl.ds(line, X, stride=Y)
            for c in range(3):
                mv[c, own, :] = mv[c, own, :] + factor * ysr[side, c]

    merged = jnp.where(even, zsr[0], pltpu.roll(zsr[1], Z - 2, 1))
    for c in range(3):
        for x in range(X):
            own = pl.ds(x * Y, Y)
            mv[c, own, :] = mv[c, own, :] + edge_term(merged, c * X + x)
    residual_out = pltpu.make_async_copy(mv, m_hbm, out_sem.at[1])
    residual_out.start()

    for sends, _, copy in first + second_set:
        @pl.when(sends)
        def _(copy=copy):
            copy.wait_send()
    strain_out.wait()
    residual_out.wait()


def shards(sizes, u, e, t, r, b):
    X, Y, Z = t.shape
    N = X * Y
    layers = sizes[2]
    assert 8 * X <= Z and Z % 128 == 0 and Y % 8 == 0
    f32 = jnp.float32
    vmem = pltpu.VMEM
    dma = pltpu.SemaphoreType.DMA
    any_space = pl.BlockSpec(memory_space=pl.ANY)
    f, m = pl.pallas_call(
        functools.partial(kernel, (X, Y, Z), sizes),
        out_shape=(
            jax.ShapeDtypeStruct((6, N, Z), f32),
            jax.ShapeDtypeStruct((3, N, Z), f32),
        ),
        in_specs=[any_space] * 5,
        out_specs=(any_space, any_space),
        scratch_shapes=[
            vmem((3, N + 2 * Y, Z), f32),
            vmem((6, N, Z), f32),
            vmem((N, Z), f32),
            vmem((N, Z), f32),
            vmem((N, Z), jnp.int32),
            vmem((N, Z), f32),
            vmem((6, N, Z), f32),
            vmem((N, Z), f32),
            vmem((6, N, Z), f32),
            vmem((3, N, Z), f32),
            vmem((6, N + 2 * Y, Z), f32),
            vmem((2, 3, X, Z), f32),
            vmem((2, 3, X, Z), f32),
            vmem((Y, Z), f32),
            vmem((max(layers - 1, 1), Y, Z), f32),
            vmem((Y, Z), f32),
            vmem((2, 3, Y, Z), f32),
            vmem((2, 3, X, Z), f32),
            vmem((2, 3, X, Z), f32),
            vmem((Y, Z), f32),
            vmem((2, Y, Z), f32),
            vmem((2, 3, Y, Z), f32),
            dma((5,)),
            dma((2,)),
            dma((2,)), dma((2,)), dma((2,)), dma((2,)),
            dma((layers,)), dma((layers,)),
            dma((2,)), dma((2,)), dma((2,)), dma((2,)), dma((2,)), dma((2,)),
        ],
        compiler_params=pltpu.CompilerParams(collective_id=0, has_side_effects=True),
        name="strain_step",
    )(
        u.reshape(3, N, Z), e.reshape(6, N, Z), t.reshape(N, Z), r.reshape(N, Z), b.reshape(N, Z)
    )
    return f.reshape(6, X, Y, Z), m.reshape(3, X, Y, Z)


def solution(mesh):
    sizes = tuple(mesh.shape[a] for a in AXES)
    field = P("gx", "gy", "gz")
    fields = P(None, "gx", "gy", "gz")
    return jax.shard_map(
        functools.partial(shards, sizes),
        mesh=mesh,
        in_specs=(fields, fields, field, field, field),
        out_specs=(fields, fields),
        check_vma=False,
    )
```

time: 68.8 us -> 15.5 us (0.23)
  the two profiles are of different devices: /device:TPU:14 before, /device:TPU:0 now
where the time goes in v1:
time: 15.5 us; the launch traced here: 15.3 us
  Pallas kernels  11.8 us (76%)
  local copies, waits for them, and re-layouts  2.9 us (19%)
  between operations  0.65 us (4%)
    pallas_call x1, Pallas kernels, shards(): pl.pallas_call(functools.partial(kernel, (X, Y, Z), sizes), out_shape=(ja...  11.8 us
    unnamed x4, local copies, waits for them, and re-layouts  2.9 us

profile of v1, /device:TPU:0, one launch (start us, length us, event | category | flops | bytes accessed | tf_op | source)
XLA Modules:
  0.0 15.3 jit_solution(6936491668118174641)
XLA Ops:
  0.6 11.8 %strain_step.1 = (f32[6,256,128]{2,1,0:T(8,128)}, f32[3,256,128]{2,1,0:T(8,128)}) custom-call(f32[3,256,128]{2,1,0:T(8,128)} %bitcast.10, f32[6,256,128]{2,1,0:T(8,128)} %bitcast.7, f32[256,128]{1,0:T(8,128)} %bitcast.11, f32[256,128]{1,0:T(8,128)} %bitcast.12, s32[256,128]{1,0:T(8,128)} %bitcast.13), custom_call_target="tpu_custom_call" | custom-call | tf_op jit(solution)/shard_map/strain_step/pallas_call | solution.py:319
  12.4 0.0 copy-start
  12.4 2.1 %copy.9 = f32[6,16,16,128]{3,2,1,0:T(8,128)} copy(f32[6,16,16,128]{3,2,1,0:T(8,128)} %bitcast.8) | data formatting | bytes 1572864
  14.6 0.0 copy-done
  14.6 0.7 %copy.10 = f32[3,16,16,128]{3,2,1,0:T(8,128)} copy(f32[3,16,16,128]{3,2,1,0:T(8,128)S(1)} %bitcast.9) | data formatting | bytes 786432
Async XLA Ops:
  12.4 2.2 %copy-start = (f32[3,256,128]{2,1,0:T(8,128)S(1)}, f32[3,256,128]{2,1,0:T(8,128)}, u32[]{:S(2)}) copy-start(f32[3,256,128]{2,1,0:T(8,128)} %get-tuple-element.5) | copy-start | bytes 1179652

commit v2 on v1

v2 whole, which is shorter than its diff:
```python
import functools

import jax
import jax.numpy as jnp
from jax import lax
from jax.experimental import pallas as pl
from jax.experimental.pallas import tpu as pltpu
from jax.sharding import PartitionSpec as P

MESH = pl.DeviceIdType.MESH
AXES = ("gx", "gy", "gz")
X_SET = (0, 2, 1)
Y_SET = (2, 3, 4)
Z_SET = (1, 4, 5)


def merge(pairs, Z):
    low, high = pairs[0], pairs[1]
    even = (lax.broadcasted_iota(jnp.int32, low.shape, 1) & 1) == 0
    return jnp.where(even, low, pltpu.roll(high, Z - 2, 1))


def edge_term(tile, q, z_edge):
    Z = tile.shape[1]
    return (pltpu.roll(tile, (Z - 2 * q) % Z, 1) if q else tile) * z_edge


def kernel(
    dims, sizes,
    u_hbm, e_hbm, t_hbm, r_hbm, b_hbm,
    fv, mv, zsr,
    uv, ev, tv, rv, bv, pv, el, nt, sp,
    yus, yur, zus, zur, zts, ztr, xur, yss, ysr, zss, xsr,
    in_sem, x_send, x_recv, y_send, y_recv, z_send, z_recv, t_send, t_recv,
    x2_send, x2_recv, y2_send, y2_recv, z2_send, z2_recv,
):
    X, Y, Z = dims
    N = X * Y
    layers = sizes[2]
    me = [lax.axis_index(a) for a in AXES]
    has = [(me[a] > 0, me[a] < sizes[a] - 1) for a in range(3)]

    def to(axis, step):
        return {AXES[axis]: me[axis] + step}

    loads = [
        pltpu.make_async_copy(src, dst, in_sem.at[i])
        for i, (src, dst) in enumerate(
            (
                (u_hbm, uv.at[:, pl.ds(Y, N), :]),
                (r_hbm, rv),
                (e_hbm, ev),
                (t_hbm, tv),
                (b_hbm, bv),
            )
        )
    ]
    for copy in loads:
        copy.start()

    barrier = pltpu.get_barrier_semaphore()
    expected = jnp.int32(0)
    for axis in range(3):
        for side, step in enumerate((-1, 1)):
            expected = expected + has[axis][side].astype(jnp.int32)

            @pl.when(has[axis][side])
            def _(axis=axis, step=step):
                pl.semaphore_signal(barrier, inc=1, device_id=to(axis, step), device_id_type=MESH)

    for d in range(2, layers):
        expected = expected + (me[2] + d < layers).astype(jnp.int32)

        @pl.when(me[2] >= d)
        def _(d=d):
            pl.semaphore_signal(barrier, inc=1, device_id=to(2, -d), device_id_type=MESH)

    plane = jnp.zeros((Y, Z), jnp.float32)
    for c in range(3):
        uv[c, pl.ds(0, Y), :] = plane
        uv[c, pl.ds(Y + N, Y), :] = plane
    for c in range(6):
        sp[c, pl.ds(0, Y), :] = plane
        sp[c, pl.ds(Y + N, Y), :] = plane
    for d in range(1, layers):
        @pl.when(me[2] < d)
        def _(d=d):
            ztr[d - 1] = plane

    for side in range(2):
        @pl.when(jnp.logical_not(has[2][side]))
        def _(side=side):
            zur[side] = plane
            zsr[side] = plane

    lane = lax.broadcasted_iota(jnp.int32, (Y, Z), 1)
    row = lax.broadcasted_iota(jnp.int32, (Y, Z), 0)
    pair = lane >> 1
    not_last = jnp.where(row < Y - 1, 0.5, 0.0).astype(jnp.float32)
    not_first = jnp.where(row > 0, 0.5, 0.0).astype(jnp.float32)
    z_first = jnp.where(lane > 0, 0.5, 0.0).astype(jnp.float32)
    z_last = jnp.where(lane < Z - 1, 0.5, 0.0).astype(jnp.float32)
    z_edge = jnp.where(lane == 0, -0.5, jnp.where(lane == Z - 1, 0.5, 0.0)).astype(jnp.float32)

    def remote(src, dst, send, recv, axis, step):
        return pltpu.make_async_remote_copy(
            src_ref=src, dst_ref=dst, send_sem=send, recv_sem=recv,
            device_id=to(axis, step), device_id_type=MESH,
        )

    def start(copies):
        for sends, _, copy in copies:
            @pl.when(sends)
            def _(copy=copy):
                copy.start()

    def arrive(copies):
        for _, receives, copy in copies:
            @pl.when(receives)
            def _(copy=copy):
                copy.wait_recv()

    def faces(axis, src, dst, send, recv):
        return [
            (has[axis][side], has[axis][1 - side], remote(
                src[side], dst.at[1 - side], send.at[side], recv.at[1 - side], axis, step))
            for side, step in enumerate((-1, 1))
        ]

    edges = (pl.ds(Y, Y), pl.ds(Y * X, Y))
    u_x = faces(0, [uv.at[:, edge, :] for edge in edges], xur, x_send, x_recv)
    u_y = faces(1, [yus.at[0], yus.at[1]], yur, y_send, y_recv)
    u_z = faces(2, [zus, zus], zur, z_send, z_recv)
    totals_down = [
        (me[2] + d < layers, me[2] >= d, remote(
            zts, ztr.at[d - 1], t_send.at[d - 1], t_recv.at[d - 1], 2, d))
        for d in range(1, layers)
    ]

    loads[0].wait()
    for side, y in enumerate((0, Y - 1)):
        for c in range(3):
            yus[side, c] = uv[c, pl.ds(Y + y, X, stride=Y), :]
    message = plane
    for x in range(X):
        for c in range(3):
            q = c * X + x
            tile = pltpu.roll(uv[c, pl.ds(Y + x * Y, Y), :], (2 * q + 1) % Z, 1)
            message = jnp.where(pair == q, tile, message)
    zus[...] = message
    pl.semaphore_wait(barrier, expected)
    start(u_z + u_x + u_y)

    loads[1].wait()
    total_depth = Z * layers
    depth = (me[2] * Z + lax.broadcasted_iota(jnp.int32, (N, Z), 1)).astype(jnp.float32)
    weight = rv[...] * (1.0 + 2.0 * depth / total_depth) / total_depth
    above_row = lax.broadcasted_iota(jnp.int32, (Z, 2 * Z), 0)
    column = lax.broadcasted_iota(jnp.int32, (Z, 2 * Z), 1)
    triangle = jnp.where(
        (above_row < column) | (column >= Z),
        1.0,
        jnp.where(above_row == column, 0.5, 0.0),
    ).astype(jnp.float32)
    sums = jnp.dot(
        weight, triangle, precision=lax.Precision.HIGHEST, preferred_element_type=jnp.float32
    )
    pv[...] = sums[:, :Z] + 1.0
    totals = sums[:, Z:]
    message = plane
    for x in range(X):
        message = jnp.where(lane == x, totals[x * Y:(x + 1) * Y], message)
    zts[...] = message
    start(totals_down)

    for copy in loads[2:]:
        copy.wait()
    for x in range(X):
        base = Y + x * Y
        own = pl.ds(x * Y, Y)
        grad = []
        for c in range(3):
            here = uv[c, pl.ds(base, Y), :]
            grad.append((
                (uv[c, pl.ds(base + Y, Y), :] - uv[c, pl.ds(base - Y, Y), :]) * 0.5,
                uv[c, pl.ds(base + 1, Y), :] * not_last - uv[c, pl.ds(base - 1, Y), :] * not_first,
                pltpu.roll(here, Z - 1, 1) * z_last - pltpu.roll(here, 1, 1) * z_first,
            ))
        el[0, own, :] = grad[0][0] - ev[0, own, :]
        el[1, own, :] = grad[1][1] - ev[1, own, :]
        el[2, own, :] = grad[2][2] - ev[2, own, :]
        el[3, own, :] = 0.5 * (grad[0][1] + grad[1][0]) - ev[3, own, :]
        el[4, own, :] = 0.5 * (grad[0][2] + grad[2][0]) - ev[4, own, :]
        el[5, own, :] = 0.5 * (grad[1][2] + grad[2][1]) - ev[5, own, :]
        nt[own, :] = -2.0 / tv[own, :]

    arrive(u_x + u_y)
    for side in range(2):
        sign = -1.0 if side == 0 else 1.0
        at = 0 if side == 0 else X - 1
        line = 0 if side == 0 else Y - 1

        @pl.when(has[0][side])
        def _(side=side, sign=sign, at=at):
            own = pl.ds(at * Y, Y)
            for c, (part, factor) in enumerate(((0, 0.5), (3, 0.25), (4, 0.25))):
                el[part, own, :] = el[part, own, :] + (sign * factor) * xur[side, c]

        @pl.when(has[1][side])
        def _(side=side, sign=sign, line=line):
            own = pl.ds(line, X, stride=Y)
            for c, (part, factor) in enumerate(((3, 0.25), (1, 0.5), (5, 0.25))):
                el[part, own, :] = el[part, own, :] + (sign * factor) * yur[side, c]

    arrive(totals_down + u_z)
    carried = plane
    for d in range(1, layers):
        carried = carried + ztr[d - 1]
    merged = merge(zur, Z)

    s_x = faces(0, [sp.at[pl.ds(0, 3), edge, :] for edge in edges], xsr, x2_send, x2_recv)
    s_y = faces(1, [yss.at[0], yss.at[1]], ysr, y2_send, y2_recv)
    s_z = faces(2, [zss, zss], zsr, z2_send, z2_recv)

    message = plane
    for step, x in enumerate([0, X - 1] + list(range(1, X - 1))):
        own = pl.ds(x * Y, Y)
        e = [el[c, own, :] for c in range(6)]
        e[4] = e[4] + 0.5 * edge_term(merged, x, z_edge)
        e[5] = e[5] + 0.5 * edge_term(merged, X + x, z_edge)
        e[2] = e[2] + edge_term(merged, 2 * X + x, z_edge)
        load = pv[own, :] + jnp.broadcast_to(carried[:, x:x + 1], (Y, Z))
        trace = e[0] + e[1] + e[2]
        third = trace * (1.0 / 3.0)
        half = [e[0] - third, e[1] - third, e[2] - third, e[3], e[4], e[5]]
        second = half[0] * half[0] + half[1] * half[1] + half[2] * half[2]
        second = second + 2.0 * (half[3] * half[3] + half[4] * half[4] + half[5] * half[5])
        weak = 2.0 + 14.0 * bv[own, :].astype(jnp.float32)
        rate = weak * jnp.exp(load * nt[own, :]) * second
        for c in range(6):
            change = rate * half[c]
            fv[c, own, :] = ev[c, own, :] + change
            e[c] = e[c] - change
        trace = e[0] + e[1] + e[2]
        stress = [
            2.0 * e[0] + trace, 2.0 * e[4], 2.0 * e[3],
            2.0 * e[1] + trace, 2.0 * e[5], 2.0 * e[2] + trace,
        ]
        for c in range(6):
            sp[c, pl.ds(Y + x * Y, Y), :] = stress[c]
        for c in range(3):
            q = c * X + x
            message = jnp.where(pair == q, pltpu.roll(stress[Z_SET[c]], (2 * q + 1) % Z, 1), message)
        if step == 1:
            start(s_x)
    zss[...] = message
    start(s_z)
    for side, y in enumerate((0, Y - 1)):
        for c in range(3):
            yss[side, c] = sp[2 + c, pl.ds(Y + y, X, stride=Y), :]
    start(s_y)

    for x in range(X):
        base = Y + x * Y
        own = pl.ds(x * Y, Y)
        for c in range(3):
            cx, cy, cz = X_SET[c], Y_SET[c], Z_SET[c]
            here = sp[cz, pl.ds(base, Y), :]
            total = (sp[cx, pl.ds(base + Y, Y), :] - sp[cx, pl.ds(base - Y, Y), :]) * 0.5
            total = total + (
                sp[cy, pl.ds(base + 1, Y), :] * not_last - sp[cy, pl.ds(base - 1, Y), :] * not_first
            )
            total = total + (pltpu.roll(here, Z - 1, 1) * z_last - pltpu.roll(here, 1, 1) * z_first)
            if c == 2:
                total = total - 0.5 * rv[own, :]
            mv[c, own, :] = total

    arrive(s_x + s_y)
    for side in range(2):
        factor = -0.5 if side == 0 else 0.5
        at = 0 if side == 0 else X - 1
        line = 0 if side == 0 else Y - 1

        @pl.when(has[0][side])
        def _(side=side, factor=factor, at=at):
            own = pl.ds(at * Y, Y)
            for c in range(3):
                mv[c, own, :] = mv[c, own, :] + factor * xsr[side, X_SET[c]]

        @pl.when(has[1][side])
        def _(side=side, factor=factor, line=line):
            own = pl.ds(line, X, stride=Y)
            for c in range(3):
                mv[c, own, :] = mv[c, own, :] + factor * ysr[side, c]

    arrive(s_z)
    for sends, _, copy in u_x + u_y + u_z + totals_down + s_x + s_y + s_z:
        @pl.when(sends)
        def _(copy=copy):
            copy.wait_send()


def finish(dims, fv, mv, zsr, f_hbm, m_hbm, mo, sem):
    X, Y, Z = dims
    N = X * Y
    strain_out = pltpu.make_async_copy(fv, f_hbm, sem.at[3])
    strain_out.start()
    lane = lax.broadcasted_iota(jnp.int32, (Y, Z), 1)
    z_edge = jnp.where(lane == 0, -0.5, jnp.where(lane == Z - 1, 0.5, 0.0)).astype(jnp.float32)
    merged = merge(zsr, Z)
    outs = []
    for c in range(3):
        for x in range(X):
            own = pl.ds(x * Y, Y)
            mo[c, own, :] = mv[c, own, :] + edge_term(merged, c * X + x, z_edge)
        outs.append(pltpu.make_async_copy(mo.at[c], m_hbm.at[c], sem.at[c]))
        outs[c].start()
    for copy in outs:
        copy.wait()
    strain_out.wait()


def shards(sizes, u, e, t, r, b):
    X, Y, Z = t.shape
    N = X * Y
    layers = sizes[2]
    assert 8 * X <= Z and Z % 128 == 0 and Y % 8 == 0
    f32 = jnp.float32
    vmem = pltpu.VMEM
    dma = pltpu.SemaphoreType.DMA
    any_space = pl.BlockSpec(memory_space=pl.ANY)
    in_vmem = pl.BlockSpec(memory_space=vmem)
    pair_sem = dma((2,))
    per_layer = dma((max(layers - 1, 1),))
    kept = pl.pallas_call(
        functools.partial(kernel, (X, Y, Z), sizes),
        out_shape=(vmem((6, N, Z), f32), vmem((3, N, Z), f32), vmem((2, Y, Z), f32)),
        in_specs=[any_space] * 5,
        out_specs=(in_vmem, in_vmem, in_vmem),
        scratch_shapes=[
            vmem((3, N + 2 * Y, Z), f32),
            vmem((6, N, Z), f32),
            vmem((N, Z), f32),
            vmem((N, Z), f32),
            vmem((N, Z), jnp.int32),
            vmem((N, Z), f32),
            vmem((6, N, Z), f32),
            vmem((N, Z), f32),
            vmem((6, N + 2 * Y, Z), f32),
            vmem((2, 3, X, Z), f32),
            vmem((2, 3, X, Z), f32),
            vmem((Y, Z), f32),
            vmem((2, Y, Z), f32),
            vmem((Y, Z), f32),
            vmem((max(layers - 1, 1), Y, Z), f32),
            vmem((2, 3, Y, Z), f32),
            vmem((2, 3, X, Z), f32),
            vmem((2, 3, X, Z), f32),
            vmem((Y, Z), f32),
            vmem((2, 3, Y, Z), f32),
            dma((5,)),
        ] + [pair_sem] * 6 + [per_layer] * 2 + [pair_sem] * 6,
        compiler_params=pltpu.CompilerParams(collective_id=0, has_side_effects=True),
        name="strain_step",
    )(
        u.reshape(3, N, Z), e.reshape(6, N, Z), t.reshape(N, Z), r.reshape(N, Z), b.reshape(N, Z)
    )
    f, m = pl.pallas_call(
        functools.partial(finish, (X, Y, Z)),
        out_shape=(jax.ShapeDtypeStruct((6, N, Z), f32), jax.ShapeDtypeStruct((3, N, Z), f32)),
        in_specs=[in_vmem] * 3,
        out_specs=(any_space, any_space),
        scratch_shapes=[vmem((3, N, Z), f32), dma((4,))],
        name="finish",
    )(*(pltpu.with_memory_space_constraint(k, vmem) for k in kept))
    return f.reshape(6, X, Y, Z), m.reshape(3, X, Y, Z)


def solution(mesh):
    sizes = tuple(mesh.shape[a] for a in AXES)
    field = P("gx", "gy", "gz")
    fields = P(None, "gx", "gy", "gz")
    return jax.shard_map(
        functools.partial(shards, sizes),
        mesh=mesh,
        in_specs=(fields, fields, field, field, field),
        out_specs=(fields, fields),
        check_vma=False,
    )
```

time: 15.5 us -> 13.1 us (0.85)
  local copies, waits for them, and re-layouts: 2.9 us -> 0 us
  Pallas kernels: 11.8 us -> 12.3 us
    unnamed x4 -> x0, local copies, waits for them, and re-layouts: 2.9 us -> none
    pallas_call x1 -> x2, Pallas kernels: 11.8 us -> 12.3 us  [the longest x1 11.2 us: shards(): pl.pallas_call(functools.partial(kernel, (X, Y, Z), sizes), out_shape=(vm...]
where the time goes in v2:
time: 13.1 us; the launch traced here: 12.9 us
  Pallas kernels  12.3 us (94%)
  between operations  0.64 us (5%)
    pallas_call x1, Pallas kernels, shards(): pl.pallas_call(functools.partial(kernel, (X, Y, Z), sizes), out_shape=(vm...  11.2 us
    pallas_call x1, Pallas kernels, shards(): pl.pallas_call(functools.partial(finish, (X, Y, Z)), out_shape=(jax.Shape...  1.04 us

profile of v2, /device:TPU:0, one launch (start us, length us, event | category | flops | bytes accessed | tf_op | source)
XLA Modules:
  0.0 12.9 jit_solution(7966445375567382751)
XLA Ops:
  0.6 11.2 %strain_step.1 = (f32[6,256,128]{2,1,0:T(8,128)S(1)}, f32[3,256,128]{2,1,0:T(8,128)S(1)}, f32[2,16,128]{2,1,0:T(8,128)S(1)}) custom-call(f32[3,256,128]{2,1,0:T(8,128)} %bitcast.8, f32[6,256,128]{2,1,0:T(8,128)} %bitcast.7, f32[256,128]{1,0:T(8,128)} %bitcast.9, f32[256,128]{1,0:T(8,128)} %bitcast.10, s32[256,128]{1,0:T(8,128)} %bitcast.11), custom_call_target="tpu_custom_call" | custom-call | tf_op jit(solution)/shard_map/strain_step/pallas_call | solution.py:335
  11.9 1.0 %finish.1 = (f32[6,256,128]{2,1,0:T(8,128)}, f32[3,256,128]{2,1,0:T(8,128)}) custom-call(f32[6,256,128]{2,1,0:T(8,128)S(1)} %get-tuple-element.7.fv, f32[3,256,128]{2,1,0:T(8,128)S(1)} %get-tuple-element.8.mv, f32[2,16,128]{2,1,0:T(8,128)S(1)} %get-tuple-element.9.zsr), custom_call_target="tpu_custom_call" | custom-call | tf_op jit(solution)/shard_map/finish/pallas_call | solution.py:368

commit v3 on v2

--- a/solution.py
+++ b/solution.py
@@ -27,10 +27,10 @@
 
 def kernel(
     dims, sizes,
-    u_hbm, e_hbm, t_hbm, r_hbm, b_hbm,
-    fv, mv, zsr,
+    u_hbm, u_rows, e_hbm, t_hbm, r_hbm, b_hbm,
+    fv, mv,
     uv, ev, tv, rv, bv, pv, el, nt, sp,
-    yus, yur, zus, zur, zts, ztr, xur, yss, ysr, zss, xsr,
+    yur, zus, zur, zts, ztr, xur, yss, ysr, zss, zsr, xsr,
     in_sem, x_send, x_recv, y_send, y_recv, z_send, z_recv, t_send, t_recv,
     x2_send, x2_recv, y2_send, y2_recv, z2_send, z2_recv,
 ):
@@ -93,6 +93,11 @@
             zur[side] = plane
             zsr[side] = plane
 
+        @pl.when(jnp.logical_not(has[1][side]))
+        def _(side=side):
+            for c in range(3):
+                yur[side, c] = jnp.zeros((X, Z), jnp.float32)
+
     lane = lax.broadcasted_iota(jnp.int32, (Y, Z), 1)
     row = lax.broadcasted_iota(jnp.int32, (Y, Z), 0)
     pair = lane >> 1
@@ -128,8 +133,8 @@
         ]
 
     edges = (pl.ds(Y, Y), pl.ds(Y * X, Y))
-    u_x = faces(0, [uv.at[:, edge, :] for edge in edges], xur, x_send, x_recv)
-    u_y = faces(1, [yus.at[0], yus.at[1]], yur, y_send, y_recv)
+    u_x = faces(0, [u_hbm.at[:, pl.ds(at, Y), :] for at in (0, N - Y)], xur, x_send, x_recv)
+    u_y = faces(1, [u_rows.at[:, :, y, :] for y in (0, Y - 1)], yur, y_send, y_recv)
     u_z = faces(2, [zus, zus], zur, z_send, z_recv)
     totals_down = [
         (me[2] + d < layers, me[2] >= d, remote(
@@ -137,10 +142,9 @@
         for d in range(1, layers)
     ]
 
+    pl.semaphore_wait(barrier, expected)
+    start(u_y + u_x)
     loads[0].wait()
-    for side, y in enumerate((0, Y - 1)):
-        for c in range(3):
-            yus[side, c] = uv[c, pl.ds(Y + y, X, stride=Y), :]
     message = plane
     for x in range(X):
         for c in range(3):
@@ -148,8 +152,7 @@
             tile = pltpu.roll(uv[c, pl.ds(Y + x * Y, Y), :], (2 * q + 1) % Z, 1)
             message = jnp.where(pair == q, tile, message)
     zus[...] = message
-    pl.semaphore_wait(barrier, expected)
-    start(u_z + u_x + u_y)
+    start(u_z)
 
     loads[1].wait()
     total_depth = Z * layers
@@ -194,11 +197,9 @@
         el[5, own, :] = 0.5 * (grad[1][2] + grad[2][1]) - ev[5, own, :]
         nt[own, :] = -2.0 / tv[own, :]
 
-    arrive(u_x + u_y)
-    for side in range(2):
-        sign = -1.0 if side == 0 else 1.0
-        at = 0 if side == 0 else X - 1
-        line = 0 if side == 0 else Y - 1
+    arrive(u_x)
+    for side, at in enumerate((0, X - 1)):
+        sign = 2.0 * side - 1.0
 
         @pl.when(has[0][side])
         def _(side=side, sign=sign, at=at):
@@ -206,13 +207,7 @@
             for c, (part, factor) in enumerate(((0, 0.5), (3, 0.25), (4, 0.25))):
                 el[part, own, :] = el[part, own, :] + (sign * factor) * xur[side, c]
 
-        @pl.when(has[1][side])
-        def _(side=side, sign=sign, line=line):
-            own = pl.ds(line, X, stride=Y)
-            for c, (part, factor) in enumerate(((3, 0.25), (1, 0.5), (5, 0.25))):
-                el[part, own, :] = el[part, own, :] + (sign * factor) * yur[side, c]
-
-    arrive(totals_down + u_z)
+    arrive(u_z + totals_down)
     carried = plane
     for d in range(1, layers):
         carried = carried + ztr[d - 1]
@@ -222,14 +217,7 @@
     s_y = faces(1, [yss.at[0], yss.at[1]], ysr, y2_send, y2_recv)
     s_z = faces(2, [zss, zss], zsr, z2_send, z2_recv)
 
-    message = plane
-    for step, x in enumerate([0, X - 1] + list(range(1, X - 1))):
-        own = pl.ds(x * Y, Y)
-        e = [el[c, own, :] for c in range(6)]
-        e[4] = e[4] + 0.5 * edge_term(merged, x, z_edge)
-        e[5] = e[5] + 0.5 * edge_term(merged, X + x, z_edge)
-        e[2] = e[2] + edge_term(merged, 2 * X + x, z_edge)
-        load = pv[own, :] + jnp.broadcast_to(carried[:, x:x + 1], (Y, Z))
+    def evolve(e, load, own):
         trace = e[0] + e[1] + e[2]
         third = trace * (1.0 / 3.0)
         half = [e[0] - third, e[1] - third, e[2] - third, e[3], e[4], e[5]]
@@ -237,28 +225,52 @@
         second = second + 2.0 * (half[3] * half[3] + half[4] * half[4] + half[5] * half[5])
         weak = 2.0 + 14.0 * bv[own, :].astype(jnp.float32)
         rate = weak * jnp.exp(load * nt[own, :]) * second
+        e = list(e)
         for c in range(6):
             change = rate * half[c]
             fv[c, own, :] = ev[c, own, :] + change
             e[c] = e[c] - change
         trace = e[0] + e[1] + e[2]
-        stress = [
+        return [
             2.0 * e[0] + trace, 2.0 * e[4], 2.0 * e[3],
             2.0 * e[1] + trace, 2.0 * e[5], 2.0 * e[2] + trace,
         ]
+
+    for x in range(X):
+        own = pl.ds(x * Y, Y)
+        e = [el[c, own, :] for c in range(6)]
+        e[4] = e[4] + 0.5 * edge_term(merged, x, z_edge)
+        e[5] = e[5] + 0.5 * edge_term(merged, X + x, z_edge)
+        e[2] = e[2] + edge_term(merged, 2 * X + x, z_edge)
+        for c in (2, 4, 5):
+            el[c, own, :] = e[c]
+        load = pv[own, :] + jnp.broadcast_to(carried[:, x:x + 1], (Y, Z))
+        pv[own, :] = load
+        stress = evolve(e, load, own)
         for c in range(6):
             sp[c, pl.ds(Y + x * Y, Y), :] = stress[c]
+
+    arrive(u_y)
+    for side, line in enumerate((0, Y - 1)):
+        sign = 2.0 * side - 1.0
+        own = pl.ds(line, X, stride=Y)
+        e = [el[c, own, :] for c in range(6)]
+        for c, (part, factor) in enumerate(((3, 0.25), (1, 0.5), (5, 0.25))):
+            e[part] = e[part] + (sign * factor) * yur[side, c]
+        stress = evolve(e, pv[own, :], own)
+        for c in range(3):
+            yss[side, c] = stress[Y_SET[c]]
+        for c in range(6):
+            sp[c, pl.ds(Y + line, X, stride=Y), :] = stress[c]
+    start(s_y + s_x)
+    message = plane
+    for x in range(X):
         for c in range(3):
             q = c * X + x
-            message = jnp.where(pair == q, pltpu.roll(stress[Z_SET[c]], (2 * q + 1) % Z, 1), message)
-        if step == 1:
-            start(s_x)
+            tile = pltpu.roll(sp[Z_SET[c], pl.ds(Y + x * Y, Y), :], (2 * q + 1) % Z, 1)
+            message = jnp.where(pair == q, tile, message)
     zss[...] = message
     start(s_z)
-    for side, y in enumerate((0, Y - 1)):
-        for c in range(3):
-            yss[side, c] = sp[2 + c, pl.ds(Y + y, X, stride=Y), :]
-    start(s_y)
 
     for x in range(X):
         base = Y + x * Y
@@ -275,49 +287,49 @@
                 total = total - 0.5 * rv[own, :]
             mv[c, own, :] = total
 
-    arrive(s_x + s_y)
-    for side in range(2):
-        factor = -0.5 if side == 0 else 0.5
-        at = 0 if side == 0 else X - 1
-        line = 0 if side == 0 else Y - 1
-
+    arrive(s_x)
+    for side, at in enumerate((0, X - 1)):
         @pl.when(has[0][side])
-        def _(side=side, factor=factor, at=at):
+        def _(side=side, at=at):
             own = pl.ds(at * Y, Y)
             for c in range(3):
-                mv[c, own, :] = mv[c, own, :] + factor * xsr[side, X_SET[c]]
-
-        @pl.when(has[1][side])
-        def _(side=side, factor=factor, line=line):
-            own = pl.ds(line, X, stride=Y)
-            for c in range(3):
-                mv[c, own, :] = mv[c, own, :] + factor * ysr[side, c]
+                mv[c, own, :] = mv[c, own, :] + (side - 0.5) * xsr[side, X_SET[c]]
 
     arrive(s_z)
-    for sends, _, copy in u_x + u_y + u_z + totals_down + s_x + s_y + s_z:
+    merged = merge(zsr, Z)
+    for c in range(3):
+        for x in range(X):
+            own = pl.ds(x * Y, Y)
+            mv[c, own, :] = mv[c, own, :] + edge_term(merged, c * X + x, z_edge)
+
+    for sends, _, copy in u_x + u_y + u_z + totals_down + s_x + s_z:
         @pl.when(sends)
         def _(copy=copy):
             copy.wait_send()
 
-
-def finish(dims, fv, mv, zsr, f_hbm, m_hbm, mo, sem):
-    X, Y, Z = dims
-    N = X * Y
-    strain_out = pltpu.make_async_copy(fv, f_hbm, sem.at[3])
-    strain_out.start()
-    lane = lax.broadcasted_iota(jnp.int32, (Y, Z), 1)
-    z_edge = jnp.where(lane == 0, -0.5, jnp.where(lane == Z - 1, 0.5, 0.0)).astype(jnp.float32)
-    merged = merge(zsr, Z)
-    outs = []
-    for c in range(3):
-        for x in range(X):
-            own = pl.ds(x * Y, Y)
-            mo[c, own, :] = mv[c, own, :] + edge_term(merged, c * X + x, z_edge)
-        outs.append(pltpu.make_async_copy(mo.at[c], m_hbm.at[c], sem.at[c]))
-        outs[c].start()
-    for copy in outs:
+    arrive(s_y)
+    for side, line in enumerate((0, Y - 1)):
+        @pl.when(has[1][side])
+        def _(side=side, line=line):
+            own = pl.ds(line, X, stride=Y)
+            for c in range(3):
+                mv[c, own, :] = mv[c, own, :] + (side - 0.5) * ysr[side, c]
+
+    for sends, _, copy in s_y:
+        @pl.when(sends)
+        def _(copy=copy):
+            copy.wait_send()
+
+
+def finish(fv, mv, f_hbm, m_hbm, sem):
+    copies = [
+        pltpu.make_async_copy(mv, m_hbm, sem.at[0]),
+        pltpu.make_async_copy(fv, f_hbm, sem.at[1]),
+    ]
+    for copy in copies:
+        copy.start()
+    for copy in copies:
         copy.wait()
-    strain_out.wait()
 
 
 def shards(sizes, u, e, t, r, b):
@@ -334,9 +346,9 @@
     per_layer = dma((max(layers - 1, 1),))
     kept = pl.pallas_call(
         functools.partial(kernel, (X, Y, Z), sizes),
-        out_shape=(vmem((6, N, Z), f32), vmem((3, N, Z), f32), vmem((2, Y, Z), f32)),
-        in_specs=[any_space] * 5,
-        out_specs=(in_vmem, in_vmem, in_vmem),
+        out_shape=(vmem((6, N, Z), f32), vmem((3, N, Z), f32)),
+        in_specs=[any_space] * 6,
+        out_specs=(in_vmem, in_vmem),
         scratch_shapes=[
             vmem((3, N + 2 * Y, Z), f32),
             vmem((6, N, Z), f32),
@@ -348,7 +360,6 @@
             vmem((N, Z), f32),
             vmem((6, N + 2 * Y, Z), f32),
             vmem((2, 3, X, Z), f32),
-            vmem((2, 3, X, Z), f32),
             vmem((Y, Z), f32),
             vmem((2, Y, Z), f32),
             vmem((Y, Z), f32),
@@ -357,20 +368,21 @@
             vmem((2, 3, X, Z), f32),
             vmem((2, 3, X, Z), f32),
             vmem((Y, Z), f32),
+            vmem((2, Y, Z), f32),
             vmem((2, 3, Y, Z), f32),
             dma((5,)),
         ] + [pair_sem] * 6 + [per_layer] * 2 + [pair_sem] * 6,
         compiler_params=pltpu.CompilerParams(collective_id=0, has_side_effects=True),
         name="strain_step",
     )(
-        u.reshape(3, N, Z), e.reshape(6, N, Z), t.reshape(N, Z), r.reshape(N, Z), b.reshape(N, Z)
+        u.reshape(3, N, Z), u, e.reshape(6, N, Z), t.reshape(N, Z), r.reshape(N, Z), b.reshape(N, Z)
     )
     f, m = pl.pallas_call(
-        functools.partial(finish, (X, Y, Z)),
+        finish,
         out_shape=(jax.ShapeDtypeStruct((6, N, Z), f32), jax.ShapeDtypeStruct((3, N, Z), f32)),
-        in_specs=[in_vmem] * 3,
+        in_specs=[in_vmem] * 2,
         out_specs=(any_space, any_space),
-        scratch_shapes=[vmem((3, N, Z), f32), dma((4,))],
+        scratch_shapes=[pair_sem],
         name="finish",
     )(*(pltpu.with_memory_space_constraint(k, vmem) for k in kept))
     return f.reshape(6, X, Y, Z), m.reshape(3, X, Y, Z)

time: 13.1 us -> 13.1 us (level)
  no operation moved by 1% of the time
where the time goes in v3:
time: 13.1 us; the launch traced here: 12.9 us
  Pallas kernels  12.3 us (94%)
  between operations  0.64 us (5%)
    pallas_call x1, Pallas kernels, shards(): pl.pallas_call(functools.partial(kernel, (X, Y, Z), sizes), out_shape=(vm...  11.2 us
    pallas_call x1, Pallas kernels, shards(): pl.pallas_call(finish, out_shape=(jax.ShapeDtypeStruct((6, N, Z), f32), j...  1.03 us

profile of v3, /device:TPU:0, one launch (start us, length us, event | category | flops | bytes accessed | tf_op | source)
XLA Modules:
  0.0 12.9 jit_solution(16730595626379154074)
XLA Ops:
  0.6 11.2 %strain_step.1 = (f32[6,256,128]{2,1,0:T(8,128)S(1)}, f32[3,256,128]{2,1,0:T(8,128)S(1)}) custom-call(f32[3,256,128]{2,1,0:T(8,128)} %bitcast.7, f32[3,16,16,128]{3,2,1,0:T(8,128)} %u_rows.1, f32[6,256,128]{2,1,0:T(8,128)} %bitcast.8, f32[256,128]{1,0:T(8,128)} %bitcast.9, f32[256,128]{1,0:T(8,128)} %bitcast.10, s32[256,128]{1,0:T(8,128)} %bitcast.11), custom_call_target="tpu_custom_call" | custom-call | tf_op jit(solution)/shard_map/strain_step/pallas_call | solution.py:347
  11.9 1.0 %finish.1 = (f32[6,256,128]{2,1,0:T(8,128)}, f32[3,256,128]{2,1,0:T(8,128)}) custom-call(f32[6,256,128]{2,1,0:T(8,128)S(1)} %get-tuple-element.6.fv, f32[3,256,128]{2,1,0:T(8,128)S(1)} %get-tuple-element.7.mv), custom_call_target="tpu_custom_call" | custom-call | tf_op jit(solution)/shard_map/finish/pallas_call | solution.py:380

commit v4 on v3

--- a/solution.py
+++ b/solution.py
@@ -93,11 +93,6 @@
             zur[side] = plane
             zsr[side] = plane
 
-        @pl.when(jnp.logical_not(has[1][side]))
-        def _(side=side):
-            for c in range(3):
-                yur[side, c] = jnp.zeros((X, Z), jnp.float32)
-
     lane = lax.broadcasted_iota(jnp.int32, (Y, Z), 1)
     row = lax.broadcasted_iota(jnp.int32, (Y, Z), 0)
     pair = lane >> 1
@@ -143,7 +138,7 @@
     ]
 
     pl.semaphore_wait(barrier, expected)
-    start(u_y + u_x)
+    start(u_x + u_y)
     loads[0].wait()
     message = plane
     for x in range(X):
@@ -197,15 +192,15 @@
         el[5, own, :] = 0.5 * (grad[1][2] + grad[2][1]) - ev[5, own, :]
         nt[own, :] = -2.0 / tv[own, :]
 
-    arrive(u_x)
-    for side, at in enumerate((0, X - 1)):
+    arrive(u_y)
+    for side, line in enumerate((0, Y - 1)):
         sign = 2.0 * side - 1.0
 
-        @pl.when(has[0][side])
-        def _(side=side, sign=sign, at=at):
-            own = pl.ds(at * Y, Y)
-            for c, (part, factor) in enumerate(((0, 0.5), (3, 0.25), (4, 0.25))):
-                el[part, own, :] = el[part, own, :] + (sign * factor) * xur[side, c]
+        @pl.when(has[1][side])
+        def _(side=side, sign=sign, line=line):
+            own = pl.ds(line, X, stride=Y)
+            for c, (part, factor) in enumerate(((3, 0.25), (1, 0.5), (5, 0.25))):
+                el[part, own, :] = el[part, own, :] + (sign * factor) * yur[side, c]
 
     arrive(u_z + totals_down)
     carried = plane
@@ -236,41 +231,44 @@
             2.0 * e[1] + trace, 2.0 * e[5], 2.0 * e[2] + trace,
         ]
 
-    for x in range(X):
+    def advance(x, message):
         own = pl.ds(x * Y, Y)
         e = [el[c, own, :] for c in range(6)]
         e[4] = e[4] + 0.5 * edge_term(merged, x, z_edge)
         e[5] = e[5] + 0.5 * edge_term(merged, X + x, z_edge)
         e[2] = e[2] + edge_term(merged, 2 * X + x, z_edge)
-        for c in (2, 4, 5):
-            el[c, own, :] = e[c]
         load = pv[own, :] + jnp.broadcast_to(carried[:, x:x + 1], (Y, Z))
-        pv[own, :] = load
         stress = evolve(e, load, own)
         for c in range(6):
             sp[c, pl.ds(Y + x * Y, Y), :] = stress[c]
-
-    arrive(u_y)
-    for side, line in enumerate((0, Y - 1)):
+        for c in range(3):
+            q = c * X + x
+            tile = pltpu.roll(stress[Z_SET[c]], (2 * q + 1) % Z, 1)
+            message = jnp.where(pair == q, tile, message)
+        return message
+
+    message = plane
+    for x in range(1, X - 1):
+        message = advance(x, message)
+    arrive(u_x)
+    for side, at in enumerate((0, X - 1)):
         sign = 2.0 * side - 1.0
-        own = pl.ds(line, X, stride=Y)
-        e = [el[c, own, :] for c in range(6)]
-        for c, (part, factor) in enumerate(((3, 0.25), (1, 0.5), (5, 0.25))):
-            e[part] = e[part] + (sign * factor) * yur[side, c]
-        stress = evolve(e, pv[own, :], own)
-        for c in range(3):
-            yss[side, c] = stress[Y_SET[c]]
-        for c in range(6):
-            sp[c, pl.ds(Y + line, X, stride=Y), :] = stress[c]
-    start(s_y + s_x)
-    message = plane
-    for x in range(X):
-        for c in range(3):
-            q = c * X + x
-            tile = pltpu.roll(sp[Z_SET[c], pl.ds(Y + x * Y, Y), :], (2 * q + 1) % Z, 1)
-            message = jnp.where(pair == q, tile, message)
+
+        @pl.when(has[0][side])
+        def _(side=side, sign=sign, at=at):
+            own = pl.ds(at * Y, Y)
+            for c, (part, factor) in enumerate(((0, 0.5), (3, 0.25), (4, 0.25))):
+                el[part, own, :] = el[part, own, :] + (sign * factor) * xur[side, c]
+
+    for x in sorted({0, X - 1}):
+        message = advance(x, message)
+    start(s_x)
     zss[...] = message
     start(s_z)
+    for side, line in enumerate((0, Y - 1)):
+        for c in range(3):
+            yss[side, c] = sp[Y_SET[c], pl.ds(Y + line, X, stride=Y), :]
+    start(s_y)
 
     for x in range(X):
         base = Y + x * Y
@@ -287,6 +285,26 @@
                 total = total - 0.5 * rv[own, :]
             mv[c, own, :] = total
 
+    arrive(s_y)
+    for side, line in enumerate((0, Y - 1)):
+        @pl.when(has[1][side])
+        def _(side=side, line=line):
+            own = pl.ds(line, X, stride=Y)
+            for c in range(3):
+                mv[c, own, :] = mv[c, own, :] + (side - 0.5) * ysr[side, c]
+
+    arrive(s_z)
+    merged = merge(zsr, Z)
+    for c in range(3):
+        for x in range(X):
+            own = pl.ds(x * Y, Y)
+            mv[c, own, :] = mv[c, own, :] + edge_term(merged, c * X + x, z_edge)
+
+    for sends, _, copy in u_x + u_y + u_z + totals_down + s_y + s_z:
+        @pl.when(sends)
+        def _(copy=copy):
+            copy.wait_send()
+
     arrive(s_x)
     for side, at in enumerate((0, X - 1)):
         @pl.when(has[0][side])
@@ -295,27 +313,7 @@
             for c in range(3):
                 mv[c, own, :] = mv[c, own, :] + (side - 0.5) * xsr[side, X_SET[c]]
 
-    arrive(s_z)
-    merged = merge(zsr, Z)
-    for c in range(3):
-        for x in range(X):
-            own = pl.ds(x * Y, Y)
-            mv[c, own, :] = mv[c, own, :] + edge_term(merged, c * X + x, z_edge)
-
-    for sends, _, copy in u_x + u_y + u_z + totals_down + s_x + s_z:
-        @pl.when(sends)
-        def _(copy=copy):
-            copy.wait_send()
-
-    arrive(s_y)
-    for side, line in enumerate((0, Y - 1)):
-        @pl.when(has[1][side])
-        def _(side=side, line=line):
-            own = pl.ds(line, X, stride=Y)
-            for c in range(3):
-                mv[c, own, :] = mv[c, own, :] + (side - 0.5) * ysr[side, c]
-
-    for sends, _, copy in s_y:
+    for sends, _, copy in s_x:
         @pl.when(sends)
         def _(copy=copy):
             copy.wait_send()

time: 13.1 us -> 12.6 us (0.962)
  Pallas kernels: 12.3 us -> 11.8 us
    pallas_call x1, Pallas kernels: 11.2 us -> 10.7 us  [shards(): pl.pallas_call(functools.partial(kernel, (X, Y, Z), sizes), out_shape=(vm...]
where the time goes in v4:
time: 12.6 us; the launch traced here: 12.4 us
  Pallas kernels  11.8 us (94%)
  between operations  0.64 us (5%)
    pallas_call x1, Pallas kernels, shards(): pl.pallas_call(functools.partial(kernel, (X, Y, Z), sizes), out_shape=(vm...  10.7 us
    pallas_call x1, Pallas kernels, shards(): pl.pallas_call(finish, out_shape=(jax.ShapeDtypeStruct((6, N, Z), f32), j...  1.03 us

profile of v4, /device:TPU:0, one launch (start us, length us, event | category | flops | bytes accessed | tf_op | source)
XLA Modules:
  0.0 12.4 jit_solution(1824642687748364780)
XLA Ops:
  0.6 10.7 %strain_step.1 = (f32[6,256,128]{2,1,0:T(8,128)S(1)}, f32[3,256,128]{2,1,0:T(8,128)S(1)}) custom-call(f32[3,256,128]{2,1,0:T(8,128)} %bitcast.7, f32[3,16,16,128]{3,2,1,0:T(8,128)} %u_rows.1, f32[6,256,128]{2,1,0:T(8,128)} %bitcast.8, f32[256,128]{1,0:T(8,128)} %bitcast.9, f32[256,128]{1,0:T(8,128)} %bitcast.10, s32[256,128]{1,0:T(8,128)} %bitcast.11), custom_call_target="tpu_custom_call" | custom-call | tf_op jit(solution)/shard_map/strain_step/pallas_call | solution.py:345
  11.4 1.0 %finish.1 = (f32[6,256,128]{2,1,0:T(8,128)}, f32[3,256,128]{2,1,0:T(8,128)}) custom-call(f32[6,256,128]{2,1,0:T(8,128)S(1)} %get-tuple-element.6.fv, f32[3,256,128]{2,1,0:T(8,128)S(1)} %get-tuple-element.7.mv), custom_call_target="tpu_custom_call" | custom-call | tf_op jit(solution)/shard_map/finish/pallas_call | solution.py:378
